TPU v7x, 256 devices: a whole 4x4x8 slice. The times are simulated.
256 devices in a mesh: dp: 32 (over y, z_lo, core), cent: 8 (over x, z_hi).
Axes of the slice: x: 4, y: 4, z: 8 (z_hi: 2, z_lo: 4; z = z_hi * 4 + z_lo), core: 2. Of those that a mesh axis runs over, the one named last changes fastest.
Arguments:
- hidden: bfloat16 [5632, 11008], P('dp', 'cent'), may hold values from -6 to 6
- residual: bfloat16 [5632, 4096], P('dp', 'cent'), may hold values from -6 to 6
- down_weight: bfloat16 [11008, 4096], P('cent', 'dp'), may hold values from -0.0546875 to 0.0546875
- gain: float32 [4096], P('cent'), may hold values from 0.1 to 1.9
- proj_weight: bfloat16 [4096, 1024], P('cent'), may hold values from -0.09375 to 0.09375
- centroids: bfloat16 [131072, 1024], P(('dp', 'cent')), may hold values from -24 to 24
Outputs:
- weighted: float32 [131072, 1024], P(('dp', 'cent'))
- counts: float32 [131072], P(('dp', 'cent'))
All inputs are finite; a program needn't handle non-finite values.
Results may differ from a plain program's by a relative error of at most 0.011.
Values may be sent and summed in bfloat16 or wider, within the bound.
A program may use at most 128 MiB of HBM per device.

v0:
```python
import math
import jax
import jax.numpy as jnp
from jax import lax
from jax.sharding import PartitionSpec as P


def body(hidden, residual, down_weight, gain, proj_weight, centroids):
    partial_layer = jnp.dot(
        hidden,
        lax.all_gather(down_weight, "dp", axis=1, tiled=True),
        preferred_element_type=jnp.float32,
    )
    layer_out = lax.psum_scatter(partial_layer, "cent", scatter_dimension=1, tiled=True)
    normed = ((layer_out + residual.astype(jnp.float32)) * gain).astype(jnp.bfloat16)
    partial_embed = jnp.dot(normed, proj_weight, preferred_element_type=jnp.float32)
    embed_width = proj_weight.shape[1]
    embed_full = lax.psum(partial_embed, "cent")
    scaled = (
        embed_full * lax.rsqrt(jnp.mean(embed_full * embed_full, axis=1, keepdims=True) + 1e-06)
    ).astype(jnp.bfloat16)
    gathered = lax.all_gather(scaled, "dp", axis=0, tiled=True)
    inverse = 1.0 / (math.sqrt(embed_width) * 0.05)
    scores = (
        lax.dot_general(
            gathered, centroids, (((1,), (1,)), ((), ())), preferred_element_type=jnp.float32
        )
        * inverse
    )
    local_max = jnp.max(scores, axis=1)
    row_max = lax.pmax(local_max, ("dp", "cent"))
    row_total = lax.psum(jnp.sum(jnp.exp(scores - row_max[:, None]), axis=1), ("dp", "cent"))
    log_total = row_max + jnp.log(row_total)
    probability = jnp.exp(scores - log_total[:, None])
    scale_up = centroids.shape[0] * lax.axis_size("dp") * lax.axis_size("cent") / gathered.shape[0]
    counts = scale_up * jnp.sum(probability, axis=0)
    prob_low = probability.astype(jnp.bfloat16)
    weighted = scale_up * lax.dot_general(
        prob_low, gathered, (((0,), (0,)), ((), ())), preferred_element_type=jnp.float32
    )
    return (weighted, counts)


def solution(mesh):
    in_specs = (
        P("dp", "cent"),
        P("dp", "cent"),
        P("cent", "dp"),
        P("cent"),
        P("cent", None),
        P(("dp", "cent"), None),
    )
    out_specs = (P(("dp", "cent"), None), P(("dp", "cent")))
    return jax.shard_map(body, mesh=mesh, in_specs=in_specs, out_specs=out_specs, check_vma=False)
```

profile of v0, /device:TPU:1, one launch (start us, length us, event | category | flops | bytes accessed | tf_op | source)
XLA Modules:
  0.0 617.1 jit_solution(13492038344672853306)
XLA Ops:
  7.2 0.0 copy-start
  7.2 0.0 copy-start.1
  7.2 0.0 copy-start.3
  7.2 0.0 copy-start.2
  7.2 0.0 all-gather.3.cloned.1.call-start
  7.3 0.7 all-gather.3.cloned.1.call-update
  7.9 0.0 reduce-scatter.2.cloned.1.call-start
  8.0 105.2 %all-gather.3.cloned.1.call-done = bf16[1376,4096]{1,0:T(8,128)(2,1)} async-done(((bf16[1376,128]{1,0:T(8,128)(2,1)}), bf16[1376,4096]{1,0:T(8,128)(2,1)}) %all-gather.3.cloned.1.call-update) | async-done | bytes 11272208 | tf_op jit(solution)/shard_map/all_gather | solution.py:11
  113.2 8.5 %fusion.11 = f32[176,4096]{1,0:T(8,128)} fusion(bf16[176,1376]{1,0:T(8,128)(2,1)} %param.6, bf16[1376,4096]{1,0:T(8,128)(2,1)} %all-gather.3.cloned.1.call-done), kind=kOutput, calls=%fused_computation.17 | convolution fusion | flops 1983905792 | bytes 14640128 | tf_op jit(solution)/shard_map/dot_general | solution.py:9
  121.7 0.0 reduce-scatter.2.cloned.1.call-update
  121.7 0.0 all-reduce.2.cloned.1.call-start
  121.8 103.8 %reduce-scatter.2.cloned.1.call-done = f32[176,512]{1,0:T(8,128)} async-done(((f32[176,4096]{1,0:T(8,128)}), f32[176,512]{1,0:T(8,128)}) %reduce-scatter.2.cloned.1.call-update) | async-done | bytes 360464 | tf_op jit(solution)/shard_map/reduce_scatter | solution.py:14
  225.6 0.0 copy-done.1
  225.6 0.0 copy-done.3
  225.6 0.0 copy-done.2
  225.6 2.2 fusion.8
  227.8 0.0 all-reduce.2.cloned.1.call-update
  227.8 0.0 all-gather.5.cloned.1.call-start
  227.8 112.2 %all-reduce.2.cloned.1.call-done = f32[176,1024]{1,0:T(8,128)} async-done(((f32[176,1024]{1,0:T(8,128)}), f32[176,1024]{1,0:T(8,128)}) %all-reduce.2.cloned.1.call-update) | async-done | bytes 720912 | tf_op jit(solution)/shard_map/psum | solution.py:18
  340.1 1.2 multiply_reduce_fusion
  341.3 2.0 multiply_convert_fusion
  343.3 0.0 all-gather.5.cloned.1.call-update
  343.3 78.9 %all-gather.5.cloned.1.call-done = bf16[5632,1024]{1,0:T(8,128)(2,1)} async-done(((bf16[176,1024]{1,0:T(8,128)(2,1)}), bf16[5632,1024]{1,0:T(8,128)(2,1)}) %all-gather.5.cloned.1.call-update) | async-done | bytes 11534352 | tf_op jit(solution)/shard_map/all_gather | solution.py:22
  422.2 0.0 copy-done
  422.2 13.2 %fusion.10 = (f32[5632]{0:T(1024)S(1)}, f32[5632,512]{0,1:T(8,128)}) fusion(bf16[5632,1024]{1,0:T(8,128)(2,1)} %all-gather.5.cloned.1.call-done, bf16[512,1024]{1,0:T(8,128)(2,1)S(1)} %copy-done), kind=kOutput, calls=%fused_computation.16 | convolution fusion | flops 5911341568 | bytes 24139776 | tf_op jit(solution)/shard_map/dot_general | solution.py:25
  435.3 76.1 %pmax.7 = f32[5632]{0:T(1024)S(1)} all-reduce(f32[5632]{0:T(1024)S(1)} %get-tuple-element.2), channel_id=1, replica_groups=mesh['dp'=32,'cent'=8] {'dp','cent'}, use_global_device_ids=true, to_apply=%region_4.0 | all-reduce | flops 5632 | bytes 45056 | tf_op jit(solution)/shard_map/pmax | solution.py:31
  511.4 6.0 exponential_reduce_fusion
  517.4 73.3 %psum.15 = f32[5632]{0:T(1024)S(1)} all-reduce(f32[5632]{0:T(1024)S(1)} %exponential_reduce_fusion), channel_id=1, replica_groups=mesh['dp'=32,'cent'=8] {'dp','cent'}, use_global_device_ids=true, to_apply=%region_6.0 | all-reduce | flops 5632 | bytes 45056 | tf_op jit(solution)/shard_map/psum | solution.py:32
  590.7 6.0 fusion
  596.7 0.6 broadcast_multiply_fusion
  597.3 13.3 %fusion.5 = f32[512,1024]{1,0:T(8,128)} fusion(bf16[5632,1024]{1,0:T(8,128)(2,1)} %all-gather.5.cloned.1.call-done, f32[5632,512]{0,1:T(8,128)} %get-tuple-element.3, f32[5632]{0:T(1024)S(1)} %log_add_fusion), kind=kOutput, calls=%fused_computation.7 | convolution fusion | flops 5911871488 | bytes 25188352 | tf_op jit(solution)/shard_map/dot_general | solution.py:38
  (2 shorter events, 0.0 us)
Async XLA Ops:
  7.2 415.0 %copy-start = (bf16[512,1024]{1,0:T(8,128)(2,1)S(1)}, bf16[512,1024]{1,0:T(8,128)(2,1)}, u32[]{:S(2)}) copy-start(bf16[512,1024]{1,0:T(8,128)(2,1)} %param.11) | copy-start | bytes 3145732
  7.2 218.4 %copy-start.1 = (bf16[512,1024]{1,0:T(8,128)(2,1)S(1)}, bf16[512,1024]{1,0:T(8,128)(2,1)}, u32[]{:S(2)}) copy-start(bf16[512,1024]{1,0:T(8,128)(2,1)} %param.10) | copy-start | bytes 3145732
  7.2 218.4 %copy-start.3 = (f32[512]{0:T(512)S(1)}, f32[512]{0:T(512)}, u32[]{:S(2)}) copy-start(f32[512]{0:T(512)} %param.9) | copy-start | bytes 6148
  7.2 218.4 %copy-start.2 = (bf16[176,512]{1,0:T(8,128)(2,1)S(1)}, bf16[176,512]{1,0:T(8,128)(2,1)}, u32[]{:S(2)}) copy-start(bf16[176,512]{1,0:T(8,128)(2,1)} %param.7) | copy-start | bytes 540676
  7.2 106.0 %all-gather.3.cloned.1.call-start = ((), (), s32[]{:S(2)}) async-start(), calls=%async_computation.1 | async-start | bytes 11624448 | tf_op jit(solution)/shard_map/all_gather | solution.py:11
  7.9 217.6 %reduce-scatter.2.cloned.1.call-start = ((), (), s32[]{:S(2)}) async-start(), calls=%async_computation.2 | async-start | bytes 3244032 | tf_op jit(solution)/shard_map/reduce_scatter | solution.py:14
  121.7 218.3 %all-reduce.2.cloned.1.call-start = ((), (), s32[]{:S(2)}) async-start(), calls=%async_computation.3 | async-start | bytes 1441792 | tf_op jit(solution)/shard_map/psum | solution.py:18
  227.8 194.4 %all-gather.5.cloned.1.call-start = ((), (), s32[]{:S(2)}) async-start(), calls=%async_computation.4 | async-start | bytes 11894784 | tf_op jit(solution)/shard_map/all_gather | solution.py:22
Sparse Core Ops, SparseCore 0:
  9.8 103.3 all-gather.2
  121.8 103.6 reduce-scatter.1
  228.8 111.2 all-reduce.1
  343.4 78.7 all-gather.4
where the time goes:
time: 618 us; the launch traced here: 617 us
  waiting for transfers between devices  401 us (65%)
  blocking collectives  149 us (24%)
  matrix products  37.1 us (6%)
  other arithmetic  15.8 us (3%)
  between operations  13.8 us (2%)
    psum x1, waiting for transfers between devices, body(): embed_full = lax.psum(partial_embed, 'cent')  112 us
    all_gather x1, waiting for transfers between devices, body(): lax.all_gather(down_weight, 'dp', axis=1, tiled=True)  105 us
    reduce_scatter x1, waiting for transfers between devices, body(): lax.psum_scatter(partial_layer, 'cent', scatter_dimension=1, tiled=True)  104 us
    all_gather x1, waiting for transfers between devices, body(): gathered = lax.all_gather(scaled, 'dp', axis=0, tiled=True)  78.9 us
    pmax x1, blocking collectives, body(): row_max = lax.pmax(local_max, ('dp', 'cent'))  76.1 us
    psum x1, blocking collectives, body(): lax.psum(jnp.sum(jnp.exp(scores - row_max[:, None]), axis=1), ('dp', 'cen...  73.3 us
    dot_general x1, matrix products, body(): lax.dot_general(prob_low, gathered, (((0,), (0,)), ((), ())), preferred_e...  13.3 us
    dot_general x1, matrix products, body(): lax.dot_general(gathered, centroids, (((1,), (1,)), ((), ())), preferred_...  13.2 us
  transfers between devices with their start and end apart: 4, of which 4 were waited for; matrix products, arithmetic and copies ran while one was open for 0% of the time, Pallas kernels for 0%

commit v1 on v0

--- a/solution.py
+++ b/solution.py
@@ -3,6 +3,12 @@
 import jax.numpy as jnp
 from jax import lax
 from jax.sharding import PartitionSpec as P
+
+
+def gather_and_add(x, axis):
+    parts = lax.all_gather(x, axis, axis=0, tiled=False)
+    acc = parts.sum(axis=0)
+    return acc
 
 
 def body(hidden, residual, down_weight, gain, proj_weight, centroids):
@@ -29,7 +35,7 @@
     )
     local_max = jnp.max(scores, axis=1)
     row_max = lax.pmax(local_max, ("dp", "cent"))
-    row_total = lax.psum(jnp.sum(jnp.exp(scores - row_max[:, None]), axis=1), ("dp", "cent"))
+    row_total = gather_and_add(jnp.sum(jnp.exp(scores - row_max[:, None]), axis=1), ("dp", "cent"))
     log_total = row_max + jnp.log(row_total)
     probability = jnp.exp(scores - log_total[:, None])
     scale_up = centroids.shape[0] * lax.axis_size("dp") * lax.axis_size("cent") / gathered.shape[0]

time: 618 us -> 1270 us (2.06)
  waiting for transfers between devices: 401 us -> 1120 us
  blocking collectives: 149 us -> 76.3 us
    all_gather x0 -> x1, waiting for transfers between devices: none -> 715 us  [gather_and_add(): parts = lax.all_gather(x, axis, axis=0, tiled=False)]
    psum x1 -> x0, blocking collectives: 73.3 us -> none  [body(): lax.psum(jnp.sum(jnp.exp(scores - row_max[:, None]), axis=1), ('dp', 'cen...]
  transfers between devices with their start and end apart: 4 -> 5, of which waited for: 4 -> 5; matrix products, arithmetic and copies ran while one was open for 0% -> 0% of each run, Pallas kernels for 0% -> 0%
where the time goes in v1:
time: 1270 us
  waiting for transfers between devices  1120 us (88%)
  blocking collectives  76.3 us (6%)
  matrix products  37.1 us (3%)
  other arithmetic  21.5 us (2%)
  between operations  13.8 us (1%)
    all_gather x1, waiting for transfers between devices, gather_and_add(): parts = lax.all_gather(x, axis, axis=0, tiled=False)  715 us
    psum x1, waiting for transfers between devices, body(): embed_full = lax.psum(partial_embed, 'cent')  112 us
    all_gather x1, waiting for transfers between devices, body(): lax.all_gather(down_weight, 'dp', axis=1, tiled=True)  105 us
    reduce_scatter x1, waiting for transfers between devices, body(): lax.psum_scatter(partial_layer, 'cent', scatter_dimension=1, tiled=True)  104 us
    all_gather x1, waiting for transfers between devices, body(): gathered = lax.all_gather(scaled, 'dp', axis=0, tiled=True)  78.8 us
    pmax x1, blocking collectives, body(): row_max = lax.pmax(local_max, ('dp', 'cent'))  76.3 us
  transfers between devices with their start and end apart: 5, of which 5 were waited for; matrix products, arithmetic and copies ran while one was open for 0% of the time, Pallas kernels for 0%

profile of v1, /device:TPU:1, one launch (start us, length us, event | category | flops | bytes accessed | tf_op | source)
XLA Modules:
  0.0 1265.0 jit_solution(9648448004968659843)
XLA Ops:
  7.2 0.0 copy-start
  7.2 0.0 copy-start.1
  7.2 0.0 copy-start.3
  7.2 0.0 copy-start.2
  7.2 0.0 all-gather.6.cloned.1.call-start
  7.3 0.7 all-gather.6.cloned.1.call-update
  7.9 0.0 reduce-scatter.2.cloned.1.call-start
  8.0 105.2 %all-gather.6.cloned.1.call-done = bf16[1376,4096]{1,0:T(8,128)(2,1)} async-done(((bf16[1376,128]{1,0:T(8,128)(2,1)}), bf16[1376,4096]{1,0:T(8,128)(2,1)}) %all-gather.6.cloned.1.call-update) | async-done | bytes 11272208 | tf_op jit(solution)/shard_map/all_gather | solution.py:17
  113.2 8.5 fusion.11
  121.7 0.0 reduce-scatter.2.cloned.1.call-update
  121.7 0.0 all-reduce.2.cloned.1.call-start
  121.8 103.8 %reduce-scatter.2.cloned.1.call-done = f32[176,512]{1,0:T(8,128)} async-done(((f32[176,4096]{1,0:T(8,128)}), f32[176,512]{1,0:T(8,128)}) %reduce-scatter.2.cloned.1.call-update) | async-done | bytes 360464 | tf_op jit(solution)/shard_map/reduce_scatter | solution.py:20
  225.6 0.0 copy-done.3
  225.6 2.2 fusion.8
  227.8 0.0 all-reduce.2.cloned.1.call-update
  227.8 0.0 all-gather.8.cloned.1.call-start
  227.8 112.2 %all-reduce.2.cloned.1.call-done = f32[176,1024]{1,0:T(8,128)} async-done(((f32[176,1024]{1,0:T(8,128)}), f32[176,1024]{1,0:T(8,128)}) %all-reduce.2.cloned.1.call-update) | async-done | bytes 720912 | tf_op jit(solution)/shard_map/psum | solution.py:24
  340.1 1.2 multiply_reduce_fusion
  341.3 2.0 multiply_convert_fusion
  343.3 0.0 all-gather.8.cloned.1.call-update
  343.3 0.0 all-gather.10.cloned.1.call-start
  343.3 78.8 %all-gather.8.cloned.1.call-done = bf16[5632,1024]{1,0:T(8,128)(2,1)} async-done(((bf16[176,1024]{1,0:T(8,128)(2,1)}), bf16[5632,1024]{1,0:T(8,128)(2,1)}) %all-gather.8.cloned.1.call-update) | async-done | bytes 11534352 | tf_op jit(solution)/shard_map/all_gather | solution.py:28
  422.2 13.2 %fusion.10 = (f32[5632]{0:T(1024)S(1)}, f32[5632,512]{0,1:T(8,128)}) fusion(bf16[5632,1024]{1,0:T(8,128)(2,1)} %all-gather.8.cloned.1.call-done, bf16[512,1024]{1,0:T(8,128)(2,1)S(1)} %copy-done), kind=kOutput, calls=%fused_computation.16 | convolution fusion | flops 5911341568 | bytes 24139776 | tf_op jit(solution)/shard_map/dot_general | solution.py:31
  435.3 76.3 %pmax.7 = f32[5632]{0:T(1024)S(1)} all-reduce(f32[5632]{0:T(1024)S(1)} %get-tuple-element.2), channel_id=1, replica_groups=mesh['dp'=32,'cent'=8] {'dp','cent'}, use_global_device_ids=true, to_apply=%region_4.0 | all-reduce | flops 5632 | bytes 45056 | tf_op jit(solution)/shard_map/pmax | solution.py:37
  511.6 6.0 exponential_reduce_fusion
  517.6 0.6 reshape.16
  518.2 0.0 all-gather.10.cloned.1.call-update
  518.3 714.6 %all-gather.10.cloned.1.call-done = f32[256,1,5632]{2,1,0:T(1,128)} async-done(((f32[1,1,5632]{2,1,0:T(1,128)}), f32[256,1,5632]{2,1,0:T(1,128)}) %all-gather.10.cloned.1.call-update) | async-done | bytes 5767184 | tf_op jit(solution)/shard_map/all_gather | solution.py:9
  1232.9 5.7 reduce_sum.38
  1238.6 6.0 fusion
  1244.6 0.6 broadcast_multiply_fusion
  1245.2 13.3 %fusion.5 = f32[512,1024]{1,0:T(8,128)} fusion(bf16[5632,1024]{1,0:T(8,128)(2,1)} %all-gather.8.cloned.1.call-done, f32[5632,512]{0,1:T(8,128)} %get-tuple-element.3, f32[5632]{0:T(1024)S(1)} %log_add_fusion), kind=kOutput, calls=%fused_computation.7 | convolution fusion | flops 5911871488 | bytes 25188352 | tf_op jit(solution)/shard_map/dot_general | solution.py:44
  (5 shorter events, 0.0 us)
Async XLA Ops:
  7.2 415.0 %copy-start = (bf16[512,1024]{1,0:T(8,128)(2,1)S(1)}, bf16[512,1024]{1,0:T(8,128)(2,1)}, u32[]{:S(2)}) copy-start(bf16[512,1024]{1,0:T(8,128)(2,1)} %param.11) | copy-start | bytes 3145732
  7.2 218.4 %copy-start.1 = (bf16[512,1024]{1,0:T(8,128)(2,1)S(1)}, bf16[512,1024]{1,0:T(8,128)(2,1)}, u32[]{:S(2)}) copy-start(bf16[512,1024]{1,0:T(8,128)(2,1)} %param.10) | copy-start | bytes 3145732
  7.2 218.4 %copy-start.3 = (f32[512]{0:T(512)S(1)}, f32[512]{0:T(512)}, u32[]{:S(2)}) copy-start(f32[512]{0:T(512)} %param.9) | copy-start | bytes 6148
  7.2 218.4 %copy-start.2 = (bf16[176,512]{1,0:T(8,128)(2,1)S(1)}, bf16[176,512]{1,0:T(8,128)(2,1)}, u32[]{:S(2)}) copy-start(bf16[176,512]{1,0:T(8,128)(2,1)} %param.7) | copy-start | bytes 540676
  7.2 106.0 %all-gather.6.cloned.1.call-start = ((), (), s32[]{:S(2)}) async-start(), calls=%async_computation.1 | async-start | bytes 11624448 | tf_op jit(solution)/shard_map/all_gather | solution.py:17
  7.9 217.6 %reduce-scatter.2.cloned.1.call-start = ((), (), s32[]{:S(2)}) async-start(), calls=%async_computation.2 | async-start | bytes 3244032 | tf_op jit(solution)/shard_map/reduce_scatter | solution.py:20
  121.7 218.3 %all-reduce.2.cloned.1.call-start = ((), (), s32[]{:S(2)}) async-start(), calls=%async_computation.3 | async-start | bytes 1441792 | tf_op jit(solution)/shard_map/psum | solution.py:24
  227.8 194.4 %all-gather.8.cloned.1.call-start = ((), (), s32[]{:S(2)}) async-start(), calls=%async_computation.4 | async-start | bytes 11894784 | tf_op jit(solution)/shard_map/all_gather | solution.py:28
  343.3 889.6 %all-gather.10.cloned.1.call-start = ((), (), s32[]{:S(2)}) async-start(), calls=%async_computation.5 | async-start | bytes 5789696 | tf_op jit(solution)/shard_map/all_gather | solution.py:9
Sparse Core Ops, SparseCore 0:
  9.8 103.3 all-gather.5
  121.8 103.6 reduce-scatter.1
  228.8 111.2 all-reduce.1
  343.4 78.7 all-gather.7
  518.4 714.4 all-gather.9
